TPU v7x, 256 devices: a whole 4x4x8 slice. The times are simulated.
256 devices in a mesh: blk: 16 (over z, core), segment: 2 (over y_hi), rep: 8 (over x, y_lo).
Axes of the slice: x: 4, y: 4 (y_hi: 2, y_lo: 2; y = y_hi * 2 + y_lo), z: 8, core: 2. Of those that a mesh axis runs over, the one named last changes fastest.
Arguments:
- features: bfloat16 [16384, 256], P('blk'), may hold values from -14 to 14
- tile_weight: bfloat16 [49152, 128, 128], P(('blk', 'segment', 'rep')), may hold values from -0.099609375 to 0.099609375
- tile_limit: int32 [49152, 128], P(('blk', 'segment', 'rep')), may hold values from 1 to 128
- tile_src: int32 [49152, 1], P(('blk', 'segment', 'rep')), may hold values from 0 to 15; in each aligned block of 192 rows (0 to 191, 192 to 383, ...) at most 24 rows name the same one
- tile_row: int32 [49152], P(('blk', 'segment', 'rep')), may hold values from 0 to 5
- tile_col: int32 [49152], P(('blk', 'segment', 'rep')), may hold values from 0 to 7
- gain_one: float32 [256], replicated, may hold values from 0.25 to 1.75
- up_one: bfloat16 [256, 1024], replicated, may hold values from -0.375 to 0.375
- down_one: bfloat16 [1024, 256], replicated, may hold values from -0.25 to 0.25
- gain_two: float32 [256], replicated, may hold values from 0.25 to 1.75
- gate_two: bfloat16 [256, 2048], P(None, ('segment', 'rep')), may hold values from -0.375 to 0.375
- up_two: bfloat16 [256, 2048], P(None, ('segment', 'rep')), may hold values from -0.375 to 0.375
- down_two: bfloat16 [256, 2048], P(None, ('segment', 'rep')), may hold values from -0.25 to 0.25
Outputs:
- readout: bfloat16 [196608, 256], P(('blk', 'segment', 'rep'))
Inputs may be any that keep to these rules, and one draw needn't show every extreme that they name: `tile_src`: among the 192 tiles of one device at most 24 name the same partition, a bound that some block reaches.
All inputs are finite; a program needn't handle non-finite values.
Results may differ from a plain program's by a relative error of at most 0.0062.
Values may be sent and summed in bfloat16 or wider, within the bound.
No kernel may reach another device: no remote copies, remote signals or barrier semaphores. Data moves between devices by JAX's collectives and lax.ppermute only.
A program may use at most 128 MiB of HBM per device.

v0:
```python
import jax
import jax.numpy as jnp
from jax import lax
from jax.sharding import PartitionSpec as P

FEATURES = 256
TILE_SIZE = 128
SRC_BLOCK = 1024
DEST_DEV = 768
TILE_COUNT = 192
SLOT_CAP = 24


def rms_scaled(values, norm_gain):
    mean_square = jnp.mean(values * values, axis=-1, keepdims=True)
    return values * lax.rsqrt(mean_square + 1e-06) * norm_gain


def local(
    features,
    tile_weight,
    tile_limit,
    tile_src,
    tile_row,
    tile_col,
    gain_one,
    up_one,
    down_one,
    gain_two,
    gate_two,
    up_two,
    down_two,
):
    row_tiles = DEST_DEV // TILE_SIZE
    col_tiles = SRC_BLOCK // TILE_SIZE
    columns = jnp.arange(TILE_SIZE, dtype=jnp.int32)
    row_ids = jnp.arange(row_tiles, dtype=jnp.int32)
    masked = jnp.where(
        columns[None, None, :] < tile_limit[:, :, None],
        tile_weight,
        jnp.zeros((), tile_weight.dtype),
    )
    sources = tile_src[:, 0]
    partitions = lax.axis_size("blk")
    part_ids = jnp.arange(partitions, dtype=jnp.int32)
    member = (sources[:, None] == part_ids[None, :]).astype(jnp.int32)
    rank_table = jnp.cumsum(member, axis=0) - 1
    rank_held = jnp.sum(rank_table * member, axis=1)
    slot_ids = jnp.arange(SLOT_CAP, dtype=jnp.int32)
    slot_match = member[:, :, None] * (rank_held[:, None, None] == slot_ids[None, None, :]).astype(
        jnp.int32
    )
    tile_ids = jnp.arange(TILE_COUNT, dtype=jnp.int32)
    slot_tile = jnp.sum(slot_match * tile_ids[:, None, None], axis=0)
    slot_live = jnp.sum(slot_match, axis=0).astype(jnp.float32)
    zero_rows = jnp.zeros((row_tiles, TILE_SIZE, FEATURES), jnp.float32)
    source_piece = lax.all_gather(features, "blk", axis=0, tiled=True)
    block_count = source_piece.shape[0] // SRC_BLOCK

    def one_block(block_step, running):
        chosen = lax.dynamic_index_in_dim(slot_tile, block_step, 0, keepdims=False)
        live_now = lax.dynamic_index_in_dim(slot_live, block_step, 0, keepdims=False)
        source_tiles = lax.dynamic_slice_in_dim(source_piece, block_step * SRC_BLOCK, SRC_BLOCK, 0)
        source_tiles = source_tiles.reshape(col_tiles, TILE_SIZE, FEATURES)
        picked = source_tiles[tile_col[chosen]]
        contrib = jnp.einsum(
            "sij,sjf->sif", masked[chosen], picked, preferred_element_type=jnp.float32
        )
        onehot = (tile_row[chosen][:, None] == row_ids[None, :]).astype(jnp.float32) * live_now[
            :, None
        ]
        return running + jnp.einsum("sr,sif->rif", onehot, contrib, precision=lax.Precision.HIGHEST)

    summed = lax.fori_loop(0, block_count, one_block, zero_rows)
    aggregated = summed.reshape(DEST_DEV, FEATURES)
    normed_one = rms_scaled(aggregated, gain_one).astype(jnp.bfloat16)
    hidden_one = jnp.maximum(
        jnp.dot(normed_one, up_one, preferred_element_type=jnp.float32), 0.0
    ).astype(jnp.bfloat16)
    section_one = aggregated + jnp.dot(hidden_one, down_one, preferred_element_type=jnp.float32)
    normed_two = rms_scaled(section_one, gain_two).astype(jnp.bfloat16)
    gate_value = jnp.dot(
        normed_two,
        lax.all_gather(gate_two, ("segment", "rep"), axis=1, tiled=True),
        preferred_element_type=jnp.float32,
    )
    up_value = jnp.dot(
        normed_two,
        lax.all_gather(up_two, ("segment", "rep"), axis=1, tiled=True),
        preferred_element_type=jnp.float32,
    )
    hidden_two = (jax.nn.silu(gate_value) * up_value).astype(jnp.bfloat16)
    branch_two = lax.dot_general(
        hidden_two,
        lax.all_gather(down_two, ("segment", "rep"), axis=1, tiled=True),
        (((1,), (1,)), ((), ())),
        preferred_element_type=jnp.float32,
    )
    return (section_one + branch_two).astype(jnp.bfloat16)


def solution(mesh):
    in_specs = (
        P("blk", None),
        P(("blk", "segment", "rep"), None, None),
        P(("blk", "segment", "rep"), None),
        P(("blk", "segment", "rep"), None),
        P(("blk", "segment", "rep")),
        P(("blk", "segment", "rep")),
        P(),
        P(),
        P(),
        P(),
        P(None, ("segment", "rep")),
        P(None, ("segment", "rep")),
        P(None, ("segment", "rep")),
    )
    out_specs = P(("blk", "segment", "rep"), None)
    return jax.shard_map(local, mesh=mesh, in_specs=in_specs, out_specs=out_specs, check_vma=False)
```

profile of v0, /device:TPU:1, one launch (start us, length us, event | category | flops | bytes accessed | tf_op | source)
XLA Modules:
  0.0 340.6 jit_solution(471552748736940421)
XLA Ops:
  13.0 7.0 %fusion.17 = bf16[192,128,128]{2,1,0:T(8,128)(2,1)} fusion(bf16[192,128,128]{2,1,0:T(8,128)(2,1)} %param.16, s32[192,128]{1,0:T(8,128)} %param.17), kind=kLoop, calls=%fused_computation.27 | loop fusion | flops 6291456 | bytes 12681216 | tf_op jit(solution)/shard_map/jit(_where)/select_n | solution.py:38
  20.0 49.2 %all-gather.5.cloned.1.call-done = bf16[16384,256]{1,0:T(8,128)(2,1)} async-done(((bf16[1024,256]{1,0:T(8,128)(2,1)}), bf16[16384,256]{1,0:T(8,128)(2,1)}) %all-gather.5.cloned.1.call-update) | async-done | bytes 8388624 | tf_op jit(solution)/shard_map/all_gather | solution.py:57
  69.2 247.6 %while.14 = (s32[]{:T(128)}, f32[6,128,256]{2,0,1:T(8,128)}, s32[16,24]{1,0:T(8,128)S(1)}, s32[192]{0:T(256)S(1)}, f32[16,24]{1,0:T(8,128)S(1)}, /*index=5*/bf16...) while((s32[]{:T(128)}, f32[6,128,256]{2,0,1:T(8,128)}, ...), condition=%wide.region_6.7_spmd.clone, body=%wide.region_5.6_spmd.clone.sunk | while | flops 258345392 | bytes 16000889 | solution.py:74
  71.7 3.5 %gather_fusion = bf16[24,128,128]{2,1,0:T(8,128)(2,1)S(1)} fusion(bf16[192,128,128]{2,1,0:T(8,128)(2,1)} %get-tuple-element.287, s32[1024]{0:T(1024)S(1)} %pad_clamp_fusion.4), kind=kCustom, calls=%fused_computation.1.clone.clone.1 | custom fusion | bytes 1572960 | tf_op jit(solution)/shard_map/while/body/eval_jaxpr/gather | solution.py:67
  78.1 6.3 %fusion.66 = f32[6,128,256]{2,0,1:T(8,128)} fusion(f32[24,128,256]{2,1,0:T(8,128)} %fusion.64, f32[6,128,256]{2,0,1:T(8,128)} %get-tuple-element.271, pred[]{:T(512)S(6)} %compare.4, f32[24]{0:T(128)S(1)} %fusion.65, s32[24]{0:T(128)S(1)} %gather_fusion.3), kind=kOutput, calls=%fused_computation.7.clone.1 | convolution fusion | flops 57016608 | bytes 4718785 | tf_op jit(solution)/shard_map/while/body/eval_jaxpr/sr,sif->rif/dot_general | solution.py:72
  86.9 3.5 %gather_fusion = bf16[24,128,128]{2,1,0:T(8,128)(2,1)S(1)} fusion(bf16[192,128,128]{2,1,0:T(8,128)(2,1)} %get-tuple-element.287, s32[1024]{0:T(1024)S(1)} %pad_clamp_fusion.4), kind=kCustom, calls=%fused_computation.1.clone.clone.1 | custom fusion | bytes 1572960 | tf_op jit(solution)/shard_map/while/body/eval_jaxpr/gather | solution.py:67
  93.3 6.6 %fusion.66 = f32[6,128,256]{2,0,1:T(8,128)} fusion(f32[24,128,256]{2,1,0:T(8,128)} %fusion.64, f32[6,128,256]{2,0,1:T(8,128)} %get-tuple-element.271, pred[]{:T(512)S(6)} %compare.4, f32[24]{0:T(128)S(1)} %fusion.65, s32[24]{0:T(128)S(1)} %gather_fusion.3), kind=kOutput, calls=%fused_computation.7.clone.1 | convolution fusion | flops 57016608 | bytes 4718785 | tf_op jit(solution)/shard_map/while/body/eval_jaxpr/sr,sif->rif/dot_general | solution.py:72
  102.5 3.5 %gather_fusion = bf16[24,128,128]{2,1,0:T(8,128)(2,1)S(1)} fusion(bf16[192,128,128]{2,1,0:T(8,128)(2,1)} %get-tuple-element.287, s32[1024]{0:T(1024)S(1)} %pad_clamp_fusion.4), kind=kCustom, calls=%fused_computation.1.clone.clone.1 | custom fusion | bytes 1572960 | tf_op jit(solution)/shard_map/while/body/eval_jaxpr/gather | solution.py:67
  108.9 6.6 %fusion.66 = f32[6,128,256]{2,0,1:T(8,128)} fusion(f32[24,128,256]{2,1,0:T(8,128)} %fusion.64, f32[6,128,256]{2,0,1:T(8,128)} %get-tuple-element.271, pred[]{:T(512)S(6)} %compare.4, f32[24]{0:T(128)S(1)} %fusion.65, s32[24]{0:T(128)S(1)} %gather_fusion.3), kind=kOutput, calls=%fused_computation.7.clone.1 | convolution fusion | flops 57016608 | bytes 4718785 | tf_op jit(solution)/shard_map/while/body/eval_jaxpr/sr,sif->rif/dot_general | solution.py:72
  118.0 3.5 %gather_fusion = bf16[24,128,128]{2,1,0:T(8,128)(2,1)S(1)} fusion(bf16[192,128,128]{2,1,0:T(8,128)(2,1)} %get-tuple-element.287, s32[1024]{0:T(1024)S(1)} %pad_clamp_fusion.4), kind=kCustom, calls=%fused_computation.1.clone.clone.1 | custom fusion | bytes 1572960 | tf_op jit(solution)/shard_map/while/body/eval_jaxpr/gather | solution.py:67
  124.4 6.6 %fusion.66 = f32[6,128,256]{2,0,1:T(8,128)} fusion(f32[24,128,256]{2,1,0:T(8,128)} %fusion.64, f32[6,128,256]{2,0,1:T(8,128)} %get-tuple-element.271, pred[]{:T(512)S(6)} %compare.4, f32[24]{0:T(128)S(1)} %fusion.65, s32[24]{0:T(128)S(1)} %gather_fusion.3), kind=kOutput, calls=%fused_computation.7.clone.1 | convolution fusion | flops 57016608 | bytes 4718785 | tf_op jit(solution)/shard_map/while/body/eval_jaxpr/sr,sif->rif/dot_general | solution.py:72
  133.4 3.5 %gather_fusion = bf16[24,128,128]{2,1,0:T(8,128)(2,1)S(1)} fusion(bf16[192,128,128]{2,1,0:T(8,128)(2,1)} %get-tuple-element.287, s32[1024]{0:T(1024)S(1)} %pad_clamp_fusion.4), kind=kCustom, calls=%fused_computation.1.clone.clone.1 | custom fusion | bytes 1572960 | tf_op jit(solution)/shard_map/while/body/eval_jaxpr/gather | solution.py:67
  139.8 6.6 %fusion.66 = f32[6,128,256]{2,0,1:T(8,128)} fusion(f32[24,128,256]{2,1,0:T(8,128)} %fusion.64, f32[6,128,256]{2,0,1:T(8,128)} %get-tuple-element.271, pred[]{:T(512)S(6)} %compare.4, f32[24]{0:T(128)S(1)} %fusion.65, s32[24]{0:T(128)S(1)} %gather_fusion.3), kind=kOutput, calls=%fused_computation.7.clone.1 | convolution fusion | flops 57016608 | bytes 4718785 | tf_op jit(solution)/shard_map/while/body/eval_jaxpr/sr,sif->rif/dot_general | solution.py:72
  148.9 3.5 %gather_fusion = bf16[24,128,128]{2,1,0:T(8,128)(2,1)S(1)} fusion(bf16[192,128,128]{2,1,0:T(8,128)(2,1)} %get-tuple-element.287, s32[1024]{0:T(1024)S(1)} %pad_clamp_fusion.4), kind=kCustom, calls=%fused_computation.1.clone.clone.1 | custom fusion | bytes 1572960 | tf_op jit(solution)/shard_map/while/body/eval_jaxpr/gather | solution.py:67
  155.3 6.6 %fusion.66 = f32[6,128,256]{2,0,1:T(8,128)} fusion(f32[24,128,256]{2,1,0:T(8,128)} %fusion.64, f32[6,128,256]{2,0,1:T(8,128)} %get-tuple-element.271, pred[]{:T(512)S(6)} %compare.4, f32[24]{0:T(128)S(1)} %fusion.65, s32[24]{0:T(128)S(1)} %gather_fusion.3), kind=kOutput, calls=%fused_computation.7.clone.1 | convolution fusion | flops 57016608 | bytes 4718785 | tf_op jit(solution)/shard_map/while/body/eval_jaxpr/sr,sif->rif/dot_general | solution.py:72
  164.4 3.5 %gather_fusion = bf16[24,128,128]{2,1,0:T(8,128)(2,1)S(1)} fusion(bf16[192,128,128]{2,1,0:T(8,128)(2,1)} %get-tuple-element.287, s32[1024]{0:T(1024)S(1)} %pad_clamp_fusion.4), kind=kCustom, calls=%fused_computation.1.clone.clone.1 | custom fusion | bytes 1572960 | tf_op jit(solution)/shard_map/while/body/eval_jaxpr/gather | solution.py:67
  170.9 6.6 %fusion.66 = f32[6,128,256]{2,0,1:T(8,128)} fusion(f32[24,128,256]{2,1,0:T(8,128)} %fusion.64, f32[6,128,256]{2,0,1:T(8,128)} %get-tuple-element.271, pred[]{:T(512)S(6)} %compare.4, f32[24]{0:T(128)S(1)} %fusion.65, s32[24]{0:T(128)S(1)} %gather_fusion.3), kind=kOutput, calls=%fused_computation.7.clone.1 | convolution fusion | flops 57016608 | bytes 4718785 | tf_op jit(solution)/shard_map/while/body/eval_jaxpr/sr,sif->rif/dot_general | solution.py:72
  179.9 3.5 %gather_fusion = bf16[24,128,128]{2,1,0:T(8,128)(2,1)S(1)} fusion(bf16[192,128,128]{2,1,0:T(8,128)(2,1)} %get-tuple-element.287, s32[1024]{0:T(1024)S(1)} %pad_clamp_fusion.4), kind=kCustom, calls=%fused_computation.1.clone.clone.1 | custom fusion | bytes 1572960 | tf_op jit(solution)/shard_map/while/body/eval_jaxpr/gather | solution.py:67
  186.3 6.6 %fusion.66 = f32[6,128,256]{2,0,1:T(8,128)} fusion(f32[24,128,256]{2,1,0:T(8,128)} %fusion.64, f32[6,128,256]{2,0,1:T(8,128)} %get-tuple-element.271, pred[]{:T(512)S(6)} %compare.4, f32[24]{0:T(128)S(1)} %fusion.65, s32[24]{0:T(128)S(1)} %gather_fusion.3), kind=kOutput, calls=%fused_computation.7.clone.1 | convolution fusion | flops 57016608 | bytes 4718785 | tf_op jit(solution)/shard_map/while/body/eval_jaxpr/sr,sif->rif/dot_general | solution.py:72
  201.9 6.6 %fusion.66 = f32[6,128,256]{2,0,1:T(8,128)} fusion(f32[24,128,256]{2,1,0:T(8,128)} %fusion.64, f32[6,128,256]{2,0,1:T(8,128)} %get-tuple-element.271, pred[]{:T(512)S(6)} %compare.4, f32[24]{0:T(128)S(1)} %fusion.65, s32[24]{0:T(128)S(1)} %gather_fusion.3), kind=kOutput, calls=%fused_computation.7.clone.1 | convolution fusion | flops 57016608 | bytes 4718785 | tf_op jit(solution)/shard_map/while/body/eval_jaxpr/sr,sif->rif/dot_general | solution.py:72
  217.3 6.6 %fusion.66 = f32[6,128,256]{2,0,1:T(8,128)} fusion(f32[24,128,256]{2,1,0:T(8,128)} %fusion.64, f32[6,128,256]{2,0,1:T(8,128)} %get-tuple-element.271, pred[]{:T(512)S(6)} %compare.4, f32[24]{0:T(128)S(1)} %fusion.65, s32[24]{0:T(128)S(1)} %gather_fusion.3), kind=kOutput, calls=%fused_computation.7.clone.1 | convolution fusion | flops 57016608 | bytes 4718785 | tf_op jit(solution)/shard_map/while/body/eval_jaxpr/sr,sif->rif/dot_general | solution.py:72
  226.4 3.5 %gather_fusion = bf16[24,128,128]{2,1,0:T(8,128)(2,1)S(1)} fusion(bf16[192,128,128]{2,1,0:T(8,128)(2,1)} %get-tuple-element.287, s32[1024]{0:T(1024)S(1)} %pad_clamp_fusion.4), kind=kCustom, calls=%fused_computation.1.clone.clone.1 | custom fusion | bytes 1572960 | tf_op jit(solution)/shard_map/while/body/eval_jaxpr/gather | solution.py:67
  232.8 6.6 %fusion.66 = f32[6,128,256]{2,0,1:T(8,128)} fusion(f32[24,128,256]{2,1,0:T(8,128)} %fusion.64, f32[6,128,256]{2,0,1:T(8,128)} %get-tuple-element.271, pred[]{:T(512)S(6)} %compare.4, f32[24]{0:T(128)S(1)} %fusion.65, s32[24]{0:T(128)S(1)} %gather_fusion.3), kind=kOutput, calls=%fused_computation.7.clone.1 | convolution fusion | flops 57016608 | bytes 4718785 | tf_op jit(solution)/shard_map/while/body/eval_jaxpr/sr,sif->rif/dot_general | solution.py:72
  241.9 3.5 %gather_fusion = bf16[24,128,128]{2,1,0:T(8,128)(2,1)S(1)} fusion(bf16[192,128,128]{2,1,0:T(8,128)(2,1)} %get-tuple-element.287, s32[1024]{0:T(1024)S(1)} %pad_clamp_fusion.4), kind=kCustom, calls=%fused_computation.1.clone.clone.1 | custom fusion | bytes 1572960 | tf_op jit(solution)/shard_map/while/body/eval_jaxpr/gather | solution.py:67
  248.3 6.6 %fusion.66 = f32[6,128,256]{2,0,1:T(8,128)} fusion(f32[24,128,256]{2,1,0:T(8,128)} %fusion.64, f32[6,128,256]{2,0,1:T(8,128)} %get-tuple-element.271, pred[]{:T(512)S(6)} %compare.4, f32[24]{0:T(128)S(1)} %fusion.65, s32[24]{0:T(128)S(1)} %gather_fusion.3), kind=kOutput, calls=%fused_computation.7.clone.1 | convolution fusion | flops 57016608 | bytes 4718785 | tf_op jit(solution)/shard_map/while/body/eval_jaxpr/sr,sif->rif/dot_general | solution.py:72
  257.4 3.5 %gather_fusion = bf16[24,128,128]{2,1,0:T(8,128)(2,1)S(1)} fusion(bf16[192,128,128]{2,1,0:T(8,128)(2,1)} %get-tuple-element.287, s32[1024]{0:T(1024)S(1)} %pad_clamp_fusion.4), kind=kCustom, calls=%fused_computation.1.clone.clone.1 | custom fusion | bytes 1572960 | tf_op jit(solution)/shard_map/while/body/eval_jaxpr/gather | solution.py:67
  263.8 6.6 %fusion.66 = f32[6,128,256]{2,0,1:T(8,128)} fusion(f32[24,128,256]{2,1,0:T(8,128)} %fusion.64, f32[6,128,256]{2,0,1:T(8,128)} %get-tuple-element.271, pred[]{:T(512)S(6)} %compare.4, f32[24]{0:T(128)S(1)} %fusion.65, s32[24]{0:T(128)S(1)} %gather_fusion.3), kind=kOutput, calls=%fused_computation.7.clone.1 | convolution fusion | flops 57016608 | bytes 4718785 | tf_op jit(solution)/shard_map/while/body/eval_jaxpr/sr,sif->rif/dot_general | solution.py:72
  279.3 6.6 %fusion.66 = f32[6,128,256]{2,0,1:T(8,128)} fusion(f32[24,128,256]{2,1,0:T(8,128)} %fusion.64, f32[6,128,256]{2,0,1:T(8,128)} %get-tuple-element.271, pred[]{:T(512)S(6)} %compare.4, f32[24]{0:T(128)S(1)} %fusion.65, s32[24]{0:T(128)S(1)} %gather_fusion.3), kind=kOutput, calls=%fused_computation.7.clone.1 | convolution fusion | flops 57016608 | bytes 4718785 | tf_op jit(solution)/shard_map/while/body/eval_jaxpr/sr,sif->rif/dot_general | solution.py:72
  294.8 6.6 %fusion.66 = f32[6,128,256]{2,0,1:T(8,128)} fusion(f32[24,128,256]{2,1,0:T(8,128)} %fusion.64, f32[6,128,256]{2,0,1:T(8,128)} %get-tuple-element.271, pred[]{:T(512)S(6)} %compare.4, f32[24]{0:T(128)S(1)} %fusion.65, s32[24]{0:T(128)S(1)} %gather_fusion.3), kind=kOutput, calls=%fused_computation.7.clone.1 | convolution fusion | flops 57016608 | bytes 4718785 | tf_op jit(solution)/shard_map/while/body/eval_jaxpr/sr,sif->rif/dot_general | solution.py:72
  310.3 6.6 %fusion.66 = f32[6,128,256]{2,0,1:T(8,128)} fusion(f32[24,128,256]{2,1,0:T(8,128)} %fusion.64, f32[6,128,256]{2,0,1:T(8,128)} %get-tuple-element.271, pred[]{:T(512)S(6)} %compare.4, f32[24]{0:T(128)S(1)} %fusion.65, s32[24]{0:T(128)S(1)} %gather_fusion.3), kind=kOutput, calls=%fused_computation.7.clone.1 | convolution fusion | flops 57016608 | bytes 4718785 | tf_op jit(solution)/shard_map/while/body/eval_jaxpr/sr,sif->rif/dot_general | solution.py:72
  322.3 5.0 %fusion.23 = f32[768,2048]{1,0:T(8,128)} fusion(bf16[256,2048]{1,0:T(8,128)(2,1)} %all-gather.7.cloned.1.call-done, f32[768,256]{0,1:T(8,128)S(1)} %get-tuple-element.208, f32[256]{0:T(256)S(1)} %copy-done.3, f32[768]{0:T(1024)S(1)} %add_rsqrt_fusion), kind=kOutput, calls=%fused_computation.41 | convolution fusion | flops 805896192 | bytes 8130560 | tf_op jit(solution)/shard_map/dot_general | solution.py:82
  327.3 5.8 %fusion.22 = bf16[768,256]{0,1:T(8,128)(2,1)S(1)} fusion(f32[768,256]{0,1:T(8,128)S(1)} %get-tuple-element.208, bf16[256,2048]{1,0:T(8,128)(2,1)} %all-gather.11.cloned.1.call-done, f32[768,2048]{1,0:T(8,128)} %fusion.23, bf16[256,2048]{1,0:T(8,128)(2,1)} %all-gather.9.cloned.1.call-done, f32[256]{0:T(256)S(1)} %copy-done.3, f32[768]{0:T(1024)S(1)} %add_rsqrt_fusion), kind=kOutput, calls=%fused_computation.34 | convolution fusion | flops 1621032960 | bytes 9572352 | tf_op jit(solution)/shard_map/dot_general | solution.py:93
  (207 shorter events, 115.9 us)
Async XLA Ops:
  6.5 313.6 %copy-start = (bf16[1024,256]{1,0:T(8,128)(2,1)S(1)}, bf16[1024,256]{1,0:T(8,128)(2,1)}, u32[]{:S(2)}) copy-start(bf16[1024,256]{1,0:T(8,128)(2,1)} %param.23) | copy-start | bytes 1572868
  6.5 62.7 %all-gather.5.cloned.1.call-start = ((), (), s32[]{:S(2)}) async-start(), calls=%async_computation | async-start | bytes 8912896 | tf_op jit(solution)/shard_map/all_gather | solution.py:57
  7.3 315.0 %all-gather.7.cloned.1.call-start = ((), (), s32[]{:S(2)}) async-start(), calls=%async_computation.1 | async-start | bytes 1114112 | tf_op jit(solution)/shard_map/all_gather | solution.py:84
  8.0 319.3 %all-gather.11.cloned.1.call-start = ((), (), s32[]{:S(2)}) async-start(), calls=%async_computation.3 | async-start | bytes 1114112 | tf_op jit(solution)/shard_map/all_gather | solution.py:95
  8.7 318.6 %all-gather.9.cloned.1.call-start = ((), (), s32[]{:S(2)}) async-start(), calls=%async_computation.2 | async-start | bytes 1114112 | tf_op jit(solution)/shard_map/all_gather | solution.py:89
  13.0 56.3 %copy-start.1 = (s32[192]{0:T(256)S(1)}, s32[192]{0:T(256)}, u32[]{:S(2)}) copy-start(s32[192]{0:T(256)} %param.19) | copy-start | bytes 2308
  13.0 56.3 %copy-start.2 = (s32[192]{0:T(256)S(1)}, s32[192]{0:T(256)}, u32[]{:S(2)}) copy-start(s32[192]{0:T(256)} %param.20) | copy-start | bytes 2308
  69.2 250.9 %copy-start.4 = (f32[256]{0:T(256)S(1)}, f32[256]{0:T(256)}, u32[]{:S(2)}) copy-start(f32[256]{0:T(256)} %param.21) | copy-start | bytes 3076
  316.9 5.4 %copy-start.3 = (f32[256]{0:T(256)S(1)}, f32[256]{0:T(256)}, u32[]{:S(2)}) copy-start(f32[256]{0:T(256)} %param.24) | copy-start | bytes 3076
Sparse Core Ops, SparseCore 0:
  9.2 60.0 all-gather.4
  70.9 55.6 all-gather.6
  128.3 68.4 all-gather.10
  198.4 68.3 all-gather.8
where the time goes:
time: 342 us; the launch traced here: 341 us
  matrix products  153 us (45%)
  local copies, waits for them, and re-layouts  109 us (32%)
  waiting for transfers between devices  51.9 us (15%)
  between operations  13.2 us (4%)
  other arithmetic  12.4 us (4%)
    dot_general x16, matrix products, one_block(): jnp.einsum('sr,sif->rif', onehot, contrib, precision=lax.Precision.HIGHEST)  105 us
    gather x16, local copies, waits for them, and re-layouts, one_block(): masked[chosen]  55.8 us
    all_gather x1, waiting for transfers between devices, local(): source_piece = lax.all_gather(features, 'blk', axis=0, tiled=True)  49.2 us
    dot_general x16, matrix products, one_block(): jnp.einsum('sij,sjf->sif', masked[chosen], picked, preferred_element_type...  34.9 us
    gather x32, local copies, waits for them, and re-layouts, one_block(): picked = source_tiles[tile_col[chosen]]  21.7 us
    dynamic_slice x16, local copies, waits for them, and re-layouts, one_block(): lax.dynamic_slice_in_dim(source_piece, block_step * SRC_BLOCK, SRC_BLOCK, 0)  17.2 us
    gather x16, local copies, waits for them, and re-layouts, one_block(): tile_row[chosen][:, None] == row_ids[None, :]  11.3 us
    select_n x1, other arithmetic, local(): jnp.where(columns[None, None, :] < tile_limit[:, :, None], tile_weight, j...  7.02 us
  transfers between devices with their start and end apart: 4, of which 1 were waited for; matrix products, arithmetic and copies ran while one was open for 79% of the time, Pallas kernels for 0%

commit v1 on v0

v1 whole, which is shorter than its diff:
```python
import jax
import jax.numpy as jnp
from jax import lax
from jax.experimental import pallas as pl
from jax.experimental.pallas import tpu as pltpu
from jax.sharding import Mesh, PartitionSpec as P


FEATURES = 256
TILE = 128
SRC = 1024
DEST = 768
TILES = 192
ROWS = DEST // TILE
COLS = SRC // TILE
HIDDEN_ONE = 1024
SHARD = 384
HALF = SHARD // 2
RING = 8
PACK = 4 * 2 * SHARD
GROUP = 4


def sort_tiles(z, core, src, row, col):
    delta = jnp.bitwise_and(src // 2 - z + RING, RING - 1)
    slot = jnp.where(delta <= 3, 2 * delta, 2 * (RING - delta) - 1)
    slot = jnp.where(delta == 4, 7, slot)
    own = src % 2 == core
    early = jnp.logical_or(slot < 5, jnp.logical_and(own, slot < 7))
    first = jnp.where(own, jnp.where(slot < 5, slot, slot + 5), slot + 5)
    second = jnp.where(slot == 7, jnp.where(own, 2, 3), slot - 5)
    key = jnp.where(early, 0, ROWS) + row
    ids = jnp.arange(TILES, dtype=jnp.int32)
    record = ids * 128 + jnp.where(early, first, second) * COLS + col
    rank = key * TILES + ids
    spot = jnp.sum((rank[None, :] < rank[:, None]).astype(jnp.int32), axis=1)
    meta = jnp.sum(jnp.where(spot[None, :] == ids[:, None], record[None, :], 0), axis=1)
    marks = jnp.arange(16, dtype=jnp.int32)
    starts = jnp.sum((key[None, :] < marks[:, None]).astype(jnp.int32), axis=1)
    return meta, jnp.where(marks == 15, core, starts)


def row_sum(run, meta_ref, starts_ref, w_ref, fbuf, begin):
    lo = starts_ref[run]
    hi = starts_ref[run + 1]

    def step(k, total):
        weights = []
        sources = []
        for j in range(GROUP):
            at = lo + GROUP * k + j
            record = meta_ref[jnp.minimum(at, hi - 1)]
            tile = w_ref[jnp.right_shift(record, 7)]
            weights.append(jnp.where(at < hi, tile, jnp.zeros_like(tile)))
            sources.append(fbuf[jnp.bitwise_and(record, 127)])
        for j in range(0, GROUP, 2):
            total = total + jnp.dot(
                jnp.concatenate(weights[j : j + 2], axis=1),
                jnp.concatenate(sources[j : j + 2], axis=0),
                preferred_element_type=jnp.float32,
            )
        return total

    return lax.fori_loop(0, (hi - lo + GROUP - 1) // GROUP, step, begin)


def first_kernel(meta_ref, starts_ref, w_ref, own_hbm, other_hbm, next_hbm, out_ref, fbuf, fsem):
    moves = [
        pltpu.make_async_copy(own_hbm, fbuf.at[pl.ds(0, 5 * COLS)], fsem.at[0]),
        pltpu.make_async_copy(other_hbm, fbuf.at[pl.ds(5 * COLS, 5 * COLS)], fsem.at[1]),
        pltpu.make_async_copy(
            next_hbm.at[pl.ds(0, 2 * COLS)], fbuf.at[pl.ds(10 * COLS, 2 * COLS)], fsem.at[2]
        ),
    ]
    for move in moves:
        move.start()
    for move in moves:
        move.wait()
    for r in range(ROWS):
        begin = jnp.zeros((TILE, FEATURES), jnp.float32)
        out_ref[r] = row_sum(r, meta_ref, starts_ref, w_ref, fbuf, begin)


def normed(values, gain):
    mean_square = jnp.mean(values * values, axis=-1, keepdims=True)
    return (values * lax.rsqrt(mean_square + 1e-06) * gain).astype(jnp.bfloat16)


def last_kernel(
    meta_ref,
    starts_ref,
    w_ref,
    tiles_hbm,
    own_hbm,
    other_hbm,
    late_hbm,
    late_other_hbm,
    up_hbm,
    down_hbm,
    gain_one_ref,
    gain_two_ref,
    in_ref,
    out_ref,
    fbuf,
    up_ref,
    down_ref,
    own_ref,
    other_ref,
    shard_ref,
    rows_ref,
    acc_ref,
    fsem,
    wsem,
):
    blocks = [
        pltpu.make_async_copy(tiles_hbm.at[pl.ds(0, 2 * COLS)], fbuf.at[pl.ds(0, 2 * COLS)], fsem.at[0]),
        pltpu.make_async_copy(late_hbm, fbuf.at[pl.ds(2 * COLS, COLS)], fsem.at[1]),
        pltpu.make_async_copy(late_other_hbm, fbuf.at[pl.ds(3 * COLS, COLS)], fsem.at[2]),
    ]
    layers = [
        pltpu.make_async_copy(up_hbm.at[:, pl.ds(h * 256, 256)], up_ref.at[h], wsem.at[h])
        for h in range(4)
    ] + [
        pltpu.make_async_copy(down_hbm, down_ref, wsem.at[4]),
        pltpu.make_async_copy(own_hbm.at[pl.ds(2 * SRC, PACK)], own_ref, wsem.at[5]),
        pltpu.make_async_copy(other_hbm.at[pl.ds(2 * SRC, PACK)], other_ref, wsem.at[6]),
    ]
    for move in blocks + layers:
        move.start()
    for move in blocks:
        move.wait()
    for r in range(ROWS):
        acc_ref[pl.ds(r * TILE, TILE)] = row_sum(
            ROWS + r, meta_ref, starts_ref, w_ref, fbuf, in_ref[r]
        )
    for move in layers:
        move.wait()
    low = starts_ref[15] == 0
    for q in range(4):
        base = 2 * SHARD * q
        for k, at in ((0, 0), (3, HALF + SHARD)):
            mine = own_ref[base + at : base + at + HALF]
            theirs = other_ref[base + at : base + at + HALF]
            shard_ref[4 * q + k, :HALF] = jnp.where(low, mine, theirs)
            shard_ref[4 * q + k, HALF:] = jnp.where(low, theirs, mine)
        shard_ref[4 * q + 1] = own_ref[base + HALF : base + HALF + SHARD]
        shard_ref[4 * q + 2] = other_ref[base + HALF : base + HALF + SHARD]

    block = 256
    spans = [pl.ds(m * block, block) for m in range(DEST // block)]
    for at in spans:
        rows_ref[at] = normed(acc_ref[at], gain_one_ref[...])

    def layer_one(h, carry):
        for at in spans:
            hidden = jnp.dot(rows_ref[at], up_ref[h], preferred_element_type=jnp.float32)
            hidden = jnp.maximum(hidden, 0.0).astype(jnp.bfloat16)
            acc_ref[at] += jnp.dot(hidden, down_ref[h], preferred_element_type=jnp.float32)
        return carry

    lax.fori_loop(0, HIDDEN_ONE // block, layer_one, 0)
    for at in spans:
        rows_ref[at] = normed(acc_ref[at], gain_two_ref[...])

    def layer_two(pair, carry):
        left = shard_ref[2 * pair]
        right = shard_ref[2 * pair + 1]
        below = jnp.concatenate([left[FEATURES:], right[FEATURES:]], axis=0)
        for at in spans:
            parts = []
            for piece in (left, right):
                both = jnp.dot(rows_ref[at], piece[:FEATURES], preferred_element_type=jnp.float32)
                gate = both[:, :TILE]
                parts.append((gate * jax.nn.sigmoid(gate) * both[:, TILE:]).astype(jnp.bfloat16))
            acc_ref[at] += jnp.dot(
                jnp.concatenate(parts, axis=1), below, preferred_element_type=jnp.float32
            )
        return carry

    lax.fori_loop(0, 8, layer_two, 0)
    for at in spans:
        out_ref[at] = acc_ref[at].astype(jnp.bfloat16)


SMEM = pl.BlockSpec(memory_space=pltpu.SMEM)
HBM = pl.BlockSpec(memory_space=pltpu.HBM)
VMEM = pl.BlockSpec(memory_space=pltpu.VMEM)
SUMS = jax.ShapeDtypeStruct((ROWS, TILE, FEATURES), jnp.float32)
PARAMS = pltpu.CompilerParams(vmem_limit_bytes=40 << 20)


def first_sums(meta, starts, masked, own, other, following):
    return pl.pallas_call(
        first_kernel,
        out_shape=SUMS,
        in_specs=[SMEM, SMEM, VMEM, HBM, HBM, HBM],
        out_specs=VMEM,
        scratch_shapes=[
            pltpu.VMEM((12 * COLS, TILE, FEATURES), jnp.bfloat16),
            pltpu.SemaphoreType.DMA((3,)),
        ],
        compiler_params=PARAMS,
        name="first_sums",
    )(meta, starts, masked, own, other, following)


def last_stage(meta, starts, masked, blocks, own, other, late, late_other, up_one, down_one, gain_one, gain_two, sums):
    return pl.pallas_call(
        last_kernel,
        out_shape=jax.ShapeDtypeStruct((DEST, FEATURES), jnp.bfloat16),
        in_specs=[SMEM, SMEM, VMEM] + [HBM] * 7 + [VMEM] * 3,
        out_specs=VMEM,
        scratch_shapes=[
            pltpu.VMEM((4 * COLS, TILE, FEATURES), jnp.bfloat16),
            pltpu.VMEM((4, FEATURES, HIDDEN_ONE // 4), jnp.bfloat16),
            pltpu.VMEM((4, HIDDEN_ONE // 4, FEATURES), jnp.bfloat16),
            pltpu.VMEM((PACK, FEATURES), jnp.bfloat16),
            pltpu.VMEM((PACK, FEATURES), jnp.bfloat16),
            pltpu.VMEM((16, SHARD, FEATURES), jnp.bfloat16),
            pltpu.VMEM((DEST, FEATURES), jnp.bfloat16),
            pltpu.VMEM((DEST, FEATURES), jnp.float32),
            pltpu.SemaphoreType.DMA((3,)),
            pltpu.SemaphoreType.DMA((7,)),
        ],
        compiler_params=PARAMS,
        name="last_stage",
    )(meta, starts, masked, blocks, own, other, late, late_other, up_one, down_one, gain_one, gain_two, sums)


UP = [(i, (i + 1) % RING) for i in range(RING)]
DOWN = [(i, (i - 1) % RING) for i in range(RING)]
SWAP = [(0, 1), (1, 0)]
X_SPLIT = [(x, (x + 1) % 4) for x in range(4)] + [(4 + x, 4 + (x - 1) % 4) for x in range(4)]
X_FAR = [(x, (x + 2) % 4) for x in range(4)]
Y_UP = [(i, (i + 1) % 4) for i in range(4)]
Y_DOWN = [(i, (i - 1) % 4) for i in range(4)]
Y_SPLIT = Y_UP + [(4 + i, 4 + (i - 1) % 4) for i in range(4)]
Y = ("yhi", "ylo")


def local(
    features,
    tile_weight,
    tile_limit,
    tile_src,
    tile_row,
    tile_col,
    gain_one,
    up_one,
    down_one,
    gain_two,
    gate_two,
    up_two,
    down_two,
):
    core = lax.axis_index("core").astype(jnp.int32)
    z = lax.axis_index("z").astype(jnp.int32)
    shard = jnp.concatenate([jnp.concatenate([gate_two, up_two], axis=1), down_two.T], axis=0)
    part = lax.dynamic_slice_in_dim(shard, core * HALF, HALF, 0)

    up1 = lax.ppermute(features, "z", UP)
    dn1 = lax.ppermute(features, "z", DOWN)
    side = lax.ppermute(shard, ("core", "x"), X_SPLIT)
    far = lax.ppermute(part, "x", X_FAR)
    columns = jnp.arange(TILE, dtype=jnp.int32)
    masked = jnp.where(
        columns[None, None, :] < tile_limit[:, :, None],
        tile_weight,
        jnp.zeros((), tile_weight.dtype),
    )
    up1, dn1, side, far, masked = lax.optimization_barrier((up1, dn1, side, far, masked))

    up2 = lax.ppermute(up1, "z", UP)
    dn2 = lax.ppermute(dn1, "z", DOWN)
    pack = jnp.concatenate([part, side, far], axis=0)
    pack1 = lax.ppermute(pack, Y, Y_UP)
    pack3 = lax.ppermute(pack, Y, Y_DOWN)
    meta, starts = sort_tiles(z, core, tile_src[:, 0], tile_row, tile_col)
    up2, dn2, pack1, pack3, meta, starts = lax.optimization_barrier((up2, dn2, pack1, pack3, meta, starts))

    up3 = lax.ppermute(up2, "z", UP)
    dn3 = lax.ppermute(dn2, "z", DOWN)
    pack2 = lax.ppermute(jnp.where(core == 0, pack1, pack3), ("core",) + Y, Y_SPLIT)
    own = jnp.concatenate([features, up1, dn1, up2, dn2], axis=0)
    other = lax.ppermute(own, "core", SWAP)
    up3, dn3, pack2, own, other = lax.optimization_barrier((up3, dn3, pack2, own, other))

    up4 = lax.ppermute(up3[: SRC // 2], "z", UP)
    dn4 = lax.ppermute(dn3[SRC // 2 :], "z", DOWN)
    own_next = jnp.concatenate([up3, dn3, pack, pack1, pack2, pack3], axis=0)
    other_next = lax.ppermute(own_next, "core", SWAP)
    late = jnp.concatenate([up4, dn4], axis=0)
    late_other = lax.ppermute(late, "core", SWAP)

    tiles = lambda a: a.reshape(-1, TILE, FEATURES)
    sums = first_sums(meta, starts, masked, tiles(own), tiles(other), tiles(own_next))
    return last_stage(
        meta,
        starts,
        masked,
        tiles(other_next),
        own_next,
        other_next,
        tiles(late),
        tiles(late_other),
        up_one,
        down_one.reshape(4, HIDDEN_ONE // 4, FEATURES),
        gain_one[None, :],
        gain_two[None, :],
        sums,
    )


def solution(mesh):
    fine = Mesh(mesh.devices.reshape(8, 2, 2, 4, 2), ("z", "core", "yhi", "x", "ylo"))
    every = ("z", "core", "yhi", "x", "ylo")
    plane = ("yhi", "x", "ylo")
    in_specs = (
        P(("z", "core"), None),
        P(every, None, None),
        P(every, None),
        P(every, None),
        P(every),
        P(every),
        P(),
        P(),
        P(),
        P(),
        P(None, plane),
        P(None, plane),
        P(None, plane),
    )
    return jax.shard_map(local, mesh=fine, in_specs=in_specs, out_specs=P(every, None), check_vma=False)
```

time: 342 us -> 92.8 us (0.27)
  matrix products: 153 us -> 0 us
  local copies, waits for them, and re-layouts: 109 us -> 5.93 us
  waiting for transfers between devices: 51.9 us -> 21 us
  starting transfers between devices: 0.12 us -> 28.9 us
  Pallas kernels: 0 us -> 26.9 us
  between operations: 13.2 us -> 0.54 us
    dot_general x35 -> x0, matrix products: 153 us -> none  [the longest x16 105 us: one_block(): jnp.einsum('sr,sif->rif', onehot, contrib, precision=lax.Precision.HIGHEST)]
    gather x64 -> x0, local copies, waits for them, and re-layouts: 88.9 us -> none  [the longest x16 55.8 us: one_block(): masked[chosen]]
    all_gather x4 -> x0, waiting for transfers between devices: 49.3 us -> none  [the longest x1 49.2 us: local(): source_piece = lax.all_gather(features, 'blk', axis=0, tiled=True)]
    ppermute x0 -> x16, starting transfers between devices: none -> 28.9 us  [the longest x1 3.94 us: local(): dn1 = lax.ppermute(features, 'z', DOWN)]
    pallas_call x0 -> x2, Pallas kernels: none -> 26.9 us  [the longest x1 13.8 us: first_sums(): pl.pallas_call(first_kernel, out_shape=SUMS, in_specs=[SMEM, SMEM, VMEM,...]
    ppermute x0 -> x16, waiting for transfers between devices: none -> 21 us  [the longest x1 6.09 us: local(): up4 = lax.ppermute(up3[:SRC // 2], 'z', UP)]
    dynamic_slice x16 -> x1, local copies, waits for them, and re-layouts: 17.2 us -> 0.01 us  [local(): part = lax.dynamic_slice_in_dim(shard, core * HALF, HALF, 0)]
    unnamed x10 -> x45, local copies, waits for them, and re-layouts: 0.03 us -> 5.8 us
  transfers between devices with their start and end apart: 4 -> 16, of which waited for: 1 -> 6; matrix products, arithmetic and copies ran while one was open for 79% -> 13% of each run, Pallas kernels for 0% -> 15%
where the time goes in v1:
time: 92.8 us; the launch traced here: 92.5 us
  starting transfers between devices  28.9 us (31%)
  Pallas kernels  26.9 us (29%)
  waiting for transfers between devices  21 us (23%)
  other arithmetic  9.18 us (10%)
  local copies, waits for them, and re-layouts  5.93 us (6%)
    pallas_call x1, Pallas kernels, first_sums(): pl.pallas_call(first_kernel, out_shape=SUMS, in_specs=[SMEM, SMEM, VMEM,...  13.8 us
    pallas_call x1, Pallas kernels, last_stage(): pl.pallas_call(last_kernel, out_shape=jax.ShapeDtypeStruct((DEST, FEATURE...  13.1 us
    select_n x1, other arithmetic, local(): jnp.where(columns[None, None, :] < tile_limit[:, :, None], tile_weight, j...  7.07 us
    ppermute x1, waiting for transfers between devices, local(): up4 = lax.ppermute(up3[:SRC // 2], 'z', UP)  6.09 us
    unnamed x45, local copies, waits for them, and re-layouts  5.8 us
    ppermute x1, waiting for transfers between devices, local(): lax.ppermute(jnp.where(core == 0, pack1, pack3), ('core',) + Y, Y_SPLIT)  4.72 us
    ppermute x1, waiting for transfers between devices, local(): up3 = lax.ppermute(up2, 'z', UP)  4.64 us
    ppermute x1, waiting for transfers between devices, local(): pack1 = lax.ppermute(pack, Y, Y_UP)  4.11 us
  transfers between devices with their start and end apart: 16, of which 6 were waited for; matrix products, arithmetic and copies ran while one was open for 13% of the time, Pallas kernels for 15%

profile of v1, /device:TPU:1, one launch (start us, length us, event | category | flops | bytes accessed | tf_op | source)
XLA Modules:
  0.0 92.5 jit_solution(15187167082978214973)
XLA Ops:
  0.0 2.5 %collective-permute-start = (bf16[1024,256]{1,0:T(8,128)(2,1)}, bf16[1024,256]{1,0:T(8,128)(2,1)}, u32[]{:S(2)}, u32[]{:S(2)}) collective-permute-start(bf16[1024,256]{1,0:T(8,128)(2,1)} %param.13), channel_id=1, source_target_pairs={{0,32},{32,64},{64,96},{96,128},{128,160},{160,192},{192,224},{224... | collective-permute-start | bytes 1572872 | tf_op jit(solution)/shard_map/ppermute | solution.py:261
  2.5 3.9 %collective-permute-start.1 = (bf16[1024,256]{1,0:T(8,128)(2,1)}, bf16[1024,256]{1,0:T(8,128)(2,1)}, u32[]{:S(2)}, u32[]{:S(2)}) collective-permute-start(bf16[1024,256]{1,0:T(8,128)(2,1)} %param.13), channel_id=1, source_target_pairs={{0,224},{32,0},{64,32},{96,64},{128,96},{160,128},{192,160},{224,1... | collective-permute-start | bytes 1572872 | tf_op jit(solution)/shard_map/ppermute | solution.py:262
  6.4 0.9 %copy.15 = bf16[256,128]{0,1:T(8,128)(2,1)S(1)} copy(bf16[256,128]{1,0:T(8,128)(2,1)} %param.25) | data formatting | bytes 131072 | tf_op args[12]
  7.3 0.9 pad_maximum_fusion.1
  8.3 2.6 %collective-permute-start.2 = (bf16[384,256]{1,0:T(8,128)(2,1)S(1)}, bf16[384,256]{1,0:T(8,128)(2,1)S(1)}, u32[]{:S(2)}, u32[]{:S(2)}) collective-permute-start(bf16[384,256]{1,0:T(8,128)(2,1)S(1)} %pad_maximum_fusion.1), channel_id=1, source_target_pairs={{0,2},{2,4},{4,6},{6,0},{16,22},{18,16},{20,18},{22,20},{1,3},{3,5... | collective-permute-start | bytes 589832 | tf_op jit(solution)/shard_map/ppermute | solution.py:263
  10.8 0.6 collective-permute-start.3
  11.4 0.7 iota_add_fusion
  12.3 7.1 %fusion.w_ref = bf16[192,128,128]{2,1,0:T(8,128)(2,1)} fusion(bf16[192,128,128]{2,1,0:T(8,128)(2,1)} %param.14, s32[192,128]{1,0:T(8,128)} %param.15), kind=kLoop, calls=%fused_computation.1 | loop fusion | flops 6291456 | bytes 12681216 | tf_op jit(solution)/shard_map/jit(_where)/select_n | solution.py:266
  19.4 0.2 convert_reduce_fusion
  19.7 2.7 %collective-permute-start.5 = (bf16[1024,256]{1,0:T(8,128)(2,1)}, bf16[1024,256]{1,0:T(8,128)(2,1)S(1)}, u32[]{:S(2)}, u32[]{:S(2)}) collective-permute-start(bf16[1024,256]{1,0:T(8,128)(2,1)} %collective-permute-done.1), channel_id=1, source_target_pairs={{0,224},{32,0},{64,32},{96,64},{128,96},{160,128},{192,160},{224,1... | collective-permute-start | bytes 1572872 | tf_op jit(solution)/shard_map/ppermute | solution.py:274
  22.4 1.4 %collective-permute-start.6 = (bf16[768,256]{1,0:T(8,128)(2,1)S(1)}, bf16[768,256]{1,0:T(8,128)(2,1)S(1)}, u32[]{:S(2)}, u32[]{:S(2)}) collective-permute-start(bf16[768,256]{1,0:T(8,128)(2,1)S(1)} %pad_maximum_fusion), channel_id=1, source_target_pairs={{0,1},{1,8},{8,9},{9,0},{2,3},{3,10},{10,11},{11,2},{4,5},{5,12},{... | collective-permute-start | bytes 1179656 | tf_op jit(solution)/shard_map/ppermute | solution.py:276
  23.8 1.5 %collective-permute-start.7 = (bf16[768,256]{1,0:T(8,128)(2,1)S(1)}, bf16[768,256]{1,0:T(8,128)(2,1)S(1)}, u32[]{:S(2)}, u32[]{:S(2)}) collective-permute-start(bf16[768,256]{1,0:T(8,128)(2,1)S(1)} %pad_maximum_fusion), channel_id=1, source_target_pairs={{0,9},{1,0},{8,1},{9,8},{2,11},{3,2},{10,3},{11,10},{4,13},{5,4},{... | collective-permute-start | bytes 1179656 | tf_op jit(solution)/shard_map/ppermute | solution.py:277
  25.5 1.1 %constant_dynamic-update-slice_fusion.3 = bf16[5120,256]{1,0:T(8,128)(2,1)S(1)} fusion(bf16[5120,256]{1,0:T(8,128)(2,1)S(1)} %constant_dynamic-update-slice_fusion.4, bf16[1024,256]{1,0:T(8,128)(2,1)} %collective-permute-done), kind=kLoop, calls=%fused_computation.11 | loop fusion | bytes 1048576
  26.6 1.1 %constant_dynamic-update-slice_fusion.2 = bf16[5120,256]{1,0:T(8,128)(2,1)S(1)} fusion(bf16[5120,256]{1,0:T(8,128)(2,1)S(1)} %constant_dynamic-update-slice_fusion.3, bf16[1024,256]{1,0:T(8,128)(2,1)} %collective-permute-done.1), kind=kLoop, calls=%fused_computation.10 | loop fusion | bytes 1048576
  27.6 4.1 %collective-permute-done.6 = bf16[768,256]{1,0:T(8,128)(2,1)S(1)} collective-permute-done((bf16[768,256]{1,0:T(8,128)(2,1)S(1)}, bf16[768,256]{1,0:T(8,128)(2,1)S(1)}, u32[]{:S(2)}, u32[]{:S(2)}) %collective-permute-start.6) | collective-permute-done | bytes 393248 | tf_op jit(solution)/shard_map/ppermute | solution.py:276
  31.8 0.7 collective-permute-done.4
  32.5 0.7 copy-done.11
  33.2 0.2 copy-done.12
  33.4 3.0 %collective-permute-start.11 = (bf16[5120,256]{1,0:T(8,128)(2,1)S(1)}, bf16[5120,256]{1,0:T(8,128)(2,1)}, u32[]{:S(2)}, u32[]{:S(2)}) collective-permute-start(bf16[5120,256]{1,0:T(8,128)(2,1)S(1)} %constant_dynamic-update-slice_fusion), channel_id=1, source_target_pairs={{0,16},{16,0},{1,17},{17,1},{2,18},{18,2},{3,19},{19,3},{4,20},{20... | collective-permute-start | bytes 7864328 | tf_op jit(solution)/shard_map/ppermute | solution.py:285
  36.5 1.5 %copy-done = bf16[5120,256]{1,0:T(8,128)(2,1)} copy-done((bf16[5120,256]{1,0:T(8,128)(2,1)}, bf16[5120,256]{1,0:T(8,128)(2,1)S(1)}, u32[]{:S(2)}) %copy-start) | copy-done | bytes 2621464
  38.0 2.6 %collective-permute-start.9 = (bf16[1024,256]{1,0:T(8,128)(2,1)}, bf16[1024,256]{1,0:T(8,128)(2,1)S(1)}, u32[]{:S(2)}, u32[]{:S(2)}) collective-permute-start(bf16[1024,256]{1,0:T(8,128)(2,1)} %copy-done.12), channel_id=1, source_target_pairs={{0,224},{32,0},{64,32},{96,64},{128,96},{160,128},{192,160},{224,1... | collective-permute-start | bytes 1572872 | tf_op jit(solution)/shard_map/ppermute | solution.py:282
  40.7 2.8 %collective-permute-start.10 = (bf16[768,256]{1,0:T(8,128)(2,1)S(1)}, bf16[768,256]{1,0:T(8,128)(2,1)S(1)}, u32[]{:S(2)}, u32[]{:S(2)}) collective-permute-start(bf16[768,256]{1,0:T(8,128)(2,1)S(1)} %broadcast_select_fusion), channel_id=1, source_target_pairs={{0,1},{1,8},{8,9},{9,0},{16,25},{17,16},{24,17},{25,24},{2,3},{3,1... | collective-permute-start | bytes 1179656 | tf_op jit(solution)/shard_map/ppermute | solution.py:283
  43.5 4.7 %collective-permute-done.10 = bf16[768,256]{1,0:T(8,128)(2,1)S(1)} collective-permute-done((bf16[768,256]{1,0:T(8,128)(2,1)S(1)}, bf16[768,256]{1,0:T(8,128)(2,1)S(1)}, u32[]{:S(2)}, u32[]{:S(2)}) %collective-permute-start.10) | collective-permute-done | bytes 393248 | tf_op jit(solution)/shard_map/ppermute | solution.py:283
  48.2 4.6 %collective-permute-done.8 = bf16[1024,256]{1,0:T(8,128)(2,1)S(1)} collective-permute-done((bf16[1024,256]{1,0:T(8,128)(2,1)}, bf16[1024,256]{1,0:T(8,128)(2,1)S(1)}, u32[]{:S(2)}, u32[]{:S(2)}) %collective-permute-start.8) | collective-permute-done | bytes 524320 | tf_op jit(solution)/shard_map/ppermute | solution.py:281
  53.2 0.9 %collective-permute-start.12 = (bf16[5120,256]{1,0:T(8,128)(2,1)S(1)}, bf16[5120,256]{1,0:T(8,128)(2,1)S(1)}, u32[]{:S(2)}, u32[]{:S(2)}) collective-permute-start(bf16[5120,256]{1,0:T(8,128)(2,1)S(1)} %constant_dynamic-update-slice_fusion.5.own_hbm), channel_id=1, source_target_pairs={{0,16},{16,0},{1,17},{17,1},{2,18},{18,2},{3,19},{19,3},{4,20},{20... | collective-permute-start | bytes 7864328 | tf_op jit(solution)/shard_map/ppermute | solution.py:291
  54.1 2.1 %collective-permute-start.13 = (bf16[512,256]{1,0:T(8,128)(2,1)S(1)}, bf16[512,256]{1,0:T(8,128)(2,1)S(1)}, u32[]{:S(2)}, u32[]{:S(2)}) collective-permute-start(bf16[512,256]{1,0:T(8,128)(2,1)S(1)} %slice.6), channel_id=1, source_target_pairs={{0,32},{32,64},{64,96},{96,128},{128,160},{160,192},{192,224},{224... | collective-permute-start | bytes 786440 | tf_op jit(solution)/shard_map/ppermute | solution.py:288
  56.2 1.0 %collective-permute-start.14 = (bf16[512,256]{1,0:T(8,128)(2,1)S(1)}, bf16[512,256]{1,0:T(8,128)(2,1)S(1)}, u32[]{:S(2)}, u32[]{:S(2)}) collective-permute-start(bf16[512,256]{1,0:T(8,128)(2,1)S(1)} %slice.7), channel_id=1, source_target_pairs={{0,224},{32,0},{64,32},{96,64},{128,96},{160,128},{192,160},{224,1... | collective-permute-start | bytes 786440 | tf_op jit(solution)/shard_map/ppermute | solution.py:289
  57.2 6.1 %collective-permute-done.13 = bf16[512,256]{1,0:T(8,128)(2,1)S(1)} collective-permute-done((bf16[512,256]{1,0:T(8,128)(2,1)S(1)}, bf16[512,256]{1,0:T(8,128)(2,1)S(1)}, u32[]{:S(2)}, u32[]{:S(2)}) %collective-permute-start.13) | collective-permute-done | bytes 262176 | tf_op jit(solution)/shard_map/ppermute | solution.py:288
  63.3 0.8 collective-permute-done.14
  64.1 1.2 %collective-permute-start.15 = (bf16[1024,256]{1,0:T(8,128)(2,1)S(1)}, bf16[1024,256]{1,0:T(8,128)(2,1)S(1)}, u32[]{:S(2)}, u32[]{:S(2)}) collective-permute-start(bf16[1024,256]{1,0:T(8,128)(2,1)S(1)} %constant_dynamic-update-slice_fusion.13), channel_id=1, source_target_pairs={{0,16},{16,0},{1,17},{17,1},{2,18},{18,2},{3,19},{19,3},{4,20},{20... | collective-permute-start | bytes 1572872 | tf_op jit(solution)/shard_map/ppermute | solution.py:293
  65.3 13.8 %first_sums.1.in_ref = f32[6,128,256]{2,1,0:T(8,128)S(1)} custom-call(s32[192]{0:T(256)S(1)} %select_reduce_fusion.meta_ref, s32[16]{0:T(128)S(1)} %compare_select_fusion.1.starts_ref, bf16[192,128,128]{2,1,0:T(8,128)(2,1)} %fusion.w_ref, bf16[40,128,256]{2,1,0:T(8,128)(2,1)S(1)} %bitcast.15, bf16[40,128,256]{2,1,0:T(8,128)(2,1)} %bitcast.9.other_hbm, ...), custom_call_target="tpu_custom_call" | custom-call | tf_op jit(solution)/shard_map/first_sums/pallas_call | solution.py:193
  79.2 13.1 %last_stage.1 = bf16[768,256]{1,0:T(8,128)(2,1)} custom-call(s32[192]{0:T(256)S(1)} %select_reduce_fusion.meta_ref, s32[16]{0:T(128)S(1)} %compare_select_fusion.1.starts_ref, bf16[192,128,128]{2,1,0:T(8,128)(2,1)S(1)} %bitcast.12, bf16[40,128,256]{2,1,0:T(8,128)(2,1)S(1)} %bitcast.14, bf16[5120,256]{1,0:T(8,128)(2,1)S(1)} %constant_dynamic-update-slice_fusion.5.own_hbm, ...), custom_call_target="tpu_custom_call" | custom-call | tf_op jit(solution)/shard_map/last_stage/pallas_call | solution.py:208
  (64 shorter events, 0.9 us)
Async XLA Ops:
  0.0 19.6 %collective-permute-start = (bf16[1024,256]{1,0:T(8,128)(2,1)}, bf16[1024,256]{1,0:T(8,128)(2,1)}, u32[]{:S(2)}, u32[]{:S(2)}) collective-permute-start(bf16[1024,256]{1,0:T(8,128)(2,1)} %param.13), channel_id=1, source_target_pairs={{0,32},{32,64},{64,96},{96,128},{128,160},{160,192},{192,224},{224... | collective-permute-start | bytes 1572872 | tf_op jit(solution)/shard_map/ppermute | solution.py:261
  2.5 17.2 %collective-permute-start.1 = (bf16[1024,256]{1,0:T(8,128)(2,1)}, bf16[1024,256]{1,0:T(8,128)(2,1)}, u32[]{:S(2)}, u32[]{:S(2)}) collective-permute-start(bf16[1024,256]{1,0:T(8,128)(2,1)} %param.13), channel_id=1, source_target_pairs={{0,224},{32,0},{64,32},{96,64},{128,96},{160,128},{192,160},{224,1... | collective-permute-start | bytes 1572872 | tf_op jit(solution)/shard_map/ppermute | solution.py:262
  8.2 11.1 %copy-start.6 = (bf16[384,256]{1,0:T(8,128)(2,1)}, bf16[384,256]{1,0:T(8,128)(2,1)S(1)}, u32[]{:S(2)}) copy-start(bf16[384,256]{1,0:T(8,128)(2,1)S(1)} %pad_maximum_fusion.1) | copy-start | bytes 589828
  8.3 11.3 %collective-permute-start.2 = (bf16[384,256]{1,0:T(8,128)(2,1)S(1)}, bf16[384,256]{1,0:T(8,128)(2,1)S(1)}, u32[]{:S(2)}, u32[]{:S(2)}) collective-permute-start(bf16[384,256]{1,0:T(8,128)(2,1)S(1)} %pad_maximum_fusion.1), channel_id=1, source_target_pairs={{0,2},{2,4},{4,6},{6,0},{16,22},{18,16},{20,18},{22,20},{1,3},{3,5... | collective-permute-start | bytes 589832 | tf_op jit(solution)/shard_map/ppermute | solution.py:263
  10.8 8.8 %collective-permute-start.3 = (bf16[192,256]{1,0:T(8,128)(2,1)S(1)}, bf16[192,256]{1,0:T(8,128)(2,1)S(1)}, u32[]{:S(2)}, u32[]{:S(2)}) collective-permute-start(bf16[192,256]{1,0:T(8,128)(2,1)S(1)} %constant_dynamic-slice_fusion), channel_id=1, source_target_pairs={{0,4},{2,6},{4,0},{6,2},{1,5},{3,7},{5,1},{7,3},{8,12},{10,14},{12... | collective-permute-start | bytes 294920 | tf_op jit(solution)/shard_map/ppermute | solution.py:264
  12.3 7.1 %copy-start.13 = (s32[192]{0:T(256)S(1)}, s32[192]{0:T(256)}, u32[]{:S(2)}) copy-start(s32[192]{0:T(256)} %param.18) | copy-start | bytes 2308
  12.3 13.2 %copy-start.10 = (bf16[1024,256]{1,0:T(8,128)(2,1)S(1)}, bf16[1024,256]{1,0:T(8,128)(2,1)}, u32[]{:S(2)}) copy-start(bf16[1024,256]{1,0:T(8,128)(2,1)} %param.13) | copy-start | bytes 1572868
  19.6 5.7 %copy-start.8 = (bf16[384,256]{1,0:T(8,128)(2,1)}, bf16[384,256]{1,0:T(8,128)(2,1)S(1)}, u32[]{:S(2)}) copy-start(bf16[384,256]{1,0:T(8,128)(2,1)S(1)} %collective-permute-done.2) | copy-start | bytes 589828
  19.6 12.8 %collective-permute-start.4 = (bf16[1024,256]{1,0:T(8,128)(2,1)}, bf16[1024,256]{1,0:T(8,128)(2,1)S(1)}, u32[]{:S(2)}, u32[]{:S(2)}) collective-permute-start(bf16[1024,256]{1,0:T(8,128)(2,1)} %collective-permute-done), channel_id=1, source_target_pairs={{0,32},{32,64},{64,96},{96,128},{128,160},{160,192},{192,224},{224... | collective-permute-start | bytes 1572872 | tf_op jit(solution)/shard_map/ppermute | solution.py:273
  19.7 12.7 %collective-permute-start.5 = (bf16[1024,256]{1,0:T(8,128)(2,1)}, bf16[1024,256]{1,0:T(8,128)(2,1)S(1)}, u32[]{:S(2)}, u32[]{:S(2)}) collective-permute-start(bf16[1024,256]{1,0:T(8,128)(2,1)} %collective-permute-done.1), channel_id=1, source_target_pairs={{0,224},{32,0},{64,32},{96,64},{128,96},{160,128},{192,160},{224,1... | collective-permute-start | bytes 1572872 | tf_op jit(solution)/shard_map/ppermute | solution.py:274
  22.4 9.3 %collective-permute-start.6 = (bf16[768,256]{1,0:T(8,128)(2,1)S(1)}, bf16[768,256]{1,0:T(8,128)(2,1)S(1)}, u32[]{:S(2)}, u32[]{:S(2)}) collective-permute-start(bf16[768,256]{1,0:T(8,128)(2,1)S(1)} %pad_maximum_fusion), channel_id=1, source_target_pairs={{0,1},{1,8},{8,9},{9,0},{2,3},{3,10},{10,11},{11,2},{4,5},{5,12},{... | collective-permute-start | bytes 1179656 | tf_op jit(solution)/shard_map/ppermute | solution.py:276
  23.8 8.0 %collective-permute-start.7 = (bf16[768,256]{1,0:T(8,128)(2,1)S(1)}, bf16[768,256]{1,0:T(8,128)(2,1)S(1)}, u32[]{:S(2)}, u32[]{:S(2)}) collective-permute-start(bf16[768,256]{1,0:T(8,128)(2,1)S(1)} %pad_maximum_fusion), channel_id=1, source_target_pairs={{0,9},{1,0},{8,1},{9,8},{2,11},{3,2},{10,3},{11,10},{4,13},{5,4},{... | collective-permute-start | bytes 1179656 | tf_op jit(solution)/shard_map/ppermute | solution.py:277
  32.4 0.8 copy-start.11
  32.4 1.0 %copy-start.12 = (bf16[1024,256]{1,0:T(8,128)(2,1)}, bf16[1024,256]{1,0:T(8,128)(2,1)S(1)}, u32[]{:S(2)}) copy-start(bf16[1024,256]{1,0:T(8,128)(2,1)S(1)} %collective-permute-done.5) | copy-start | bytes 1572868
  33.4 19.4 %collective-permute-start.11 = (bf16[5120,256]{1,0:T(8,128)(2,1)S(1)}, bf16[5120,256]{1,0:T(8,128)(2,1)}, u32[]{:S(2)}, u32[]{:S(2)}) collective-permute-start(bf16[5120,256]{1,0:T(8,128)(2,1)S(1)} %constant_dynamic-update-slice_fusion), channel_id=1, source_target_pairs={{0,16},{16,0},{1,17},{17,1},{2,18},{18,2},{3,19},{19,3},{4,20},{20... | collective-permute-start | bytes 7864328 | tf_op jit(solution)/shard_map/ppermute | solution.py:285
  36.5 1.5 %copy-start = (bf16[5120,256]{1,0:T(8,128)(2,1)}, bf16[5120,256]{1,0:T(8,128)(2,1)S(1)}, u32[]{:S(2)}) copy-start(bf16[5120,256]{1,0:T(8,128)(2,1)S(1)} %constant_dynamic-update-slice_fusion) | copy-start | bytes 7864324
  38.0 15.0 %copy-start.7 = (bf16[384,256]{1,0:T(8,128)(2,1)S(1)}, bf16[384,256]{1,0:T(8,128)(2,1)}, u32[]{:S(2)}) copy-start(bf16[384,256]{1,0:T(8,128)(2,1)} %copy-done.6) | copy-start | bytes 589828
  38.0 15.0 %copy-start.9 = (bf16[384,256]{1,0:T(8,128)(2,1)S(1)}, bf16[384,256]{1,0:T(8,128)(2,1)}, u32[]{:S(2)}) copy-start(bf16[384,256]{1,0:T(8,128)(2,1)} %copy-done.8) | copy-start | bytes 589828
  38.0 14.9 %collective-permute-start.8 = (bf16[1024,256]{1,0:T(8,128)(2,1)}, bf16[1024,256]{1,0:T(8,128)(2,1)S(1)}, u32[]{:S(2)}, u32[]{:S(2)}) collective-permute-start(bf16[1024,256]{1,0:T(8,128)(2,1)} %copy-done.11), channel_id=1, source_target_pairs={{0,32},{32,64},{64,96},{96,128},{128,160},{160,192},{192,224},{224... | collective-permute-start | bytes 1572872 | tf_op jit(solution)/shard_map/ppermute | solution.py:281
  38.0 14.8 %collective-permute-start.9 = (bf16[1024,256]{1,0:T(8,128)(2,1)}, bf16[1024,256]{1,0:T(8,128)(2,1)S(1)}, u32[]{:S(2)}, u32[]{:S(2)}) collective-permute-start(bf16[1024,256]{1,0:T(8,128)(2,1)} %copy-done.12), channel_id=1, source_target_pairs={{0,224},{32,0},{64,32},{96,64},{128,96},{160,128},{192,160},{224,1... | collective-permute-start | bytes 1572872 | tf_op jit(solution)/shard_map/ppermute | solution.py:282
  40.7 7.5 %collective-permute-start.10 = (bf16[768,256]{1,0:T(8,128)(2,1)S(1)}, bf16[768,256]{1,0:T(8,128)(2,1)S(1)}, u32[]{:S(2)}, u32[]{:S(2)}) collective-permute-start(bf16[768,256]{1,0:T(8,128)(2,1)S(1)} %broadcast_select_fusion), channel_id=1, source_target_pairs={{0,1},{1,8},{8,9},{9,0},{16,25},{17,16},{24,17},{25,24},{2,3},{3,1... | collective-permute-start | bytes 1179656 | tf_op jit(solution)/shard_map/ppermute | solution.py:283
  53.0 12.3 %copy-start.1 = (bf16[5120,256]{1,0:T(8,128)(2,1)S(1)}, bf16[5120,256]{1,0:T(8,128)(2,1)}, u32[]{:S(2)}) copy-start(bf16[5120,256]{1,0:T(8,128)(2,1)} %copy-done) | copy-start | bytes 7864324
  53.2 26.0 %collective-permute-start.12 = (bf16[5120,256]{1,0:T(8,128)(2,1)S(1)}, bf16[5120,256]{1,0:T(8,128)(2,1)S(1)}, u32[]{:S(2)}, u32[]{:S(2)}) collective-permute-start(bf16[5120,256]{1,0:T(8,128)(2,1)S(1)} %constant_dynamic-update-slice_fusion.5.own_hbm), channel_id=1, source_target_pairs={{0,16},{16,0},{1,17},{17,1},{2,18},{18,2},{3,19},{19,3},{4,20},{20... | collective-permute-start | bytes 7864328 | tf_op jit(solution)/shard_map/ppermute | solution.py:291
  54.1 9.1 %collective-permute-start.13 = (bf16[512,256]{1,0:T(8,128)(2,1)S(1)}, bf16[512,256]{1,0:T(8,128)(2,1)S(1)}, u32[]{:S(2)}, u32[]{:S(2)}) collective-permute-start(bf16[512,256]{1,0:T(8,128)(2,1)S(1)} %slice.6), channel_id=1, source_target_pairs={{0,32},{32,64},{64,96},{96,128},{128,160},{160,192},{192,224},{224... | collective-permute-start | bytes 786440 | tf_op jit(solution)/shard_map/ppermute | solution.py:288
  56.2 7.8 %collective-permute-start.14 = (bf16[512,256]{1,0:T(8,128)(2,1)S(1)}, bf16[512,256]{1,0:T(8,128)(2,1)S(1)}, u32[]{:S(2)}, u32[]{:S(2)}) collective-permute-start(bf16[512,256]{1,0:T(8,128)(2,1)S(1)} %slice.7), channel_id=1, source_target_pairs={{0,224},{32,0},{64,32},{96,64},{128,96},{160,128},{192,160},{224,1... | collective-permute-start | bytes 786440 | tf_op jit(solution)/shard_map/ppermute | solution.py:289
  64.1 15.1 %collective-permute-start.15 = (bf16[1024,256]{1,0:T(8,128)(2,1)S(1)}, bf16[1024,256]{1,0:T(8,128)(2,1)S(1)}, u32[]{:S(2)}, u32[]{:S(2)}) collective-permute-start(bf16[1024,256]{1,0:T(8,128)(2,1)S(1)} %constant_dynamic-update-slice_fusion.13), channel_id=1, source_target_pairs={{0,16},{16,0},{1,17},{17,1},{2,18},{18,2},{3,19},{19,3},{4,20},{20... | collective-permute-start | bytes 1572872 | tf_op jit(solution)/shard_map/ppermute | solution.py:293
  65.3 13.9 %slice-start = ((s8[6291456]{0:T(1024)(128)(4,1)}), s8[4194304]{0:T(1024)(128)(4,1)S(1)}, s32[]{:S(2)}) async-start(s8[6291456]{0:T(1024)(128)(4,1)} %bitcast.11), calls=%async_computation | async-start | bytes 8388608
  65.3 13.9 %slice-start.1 = ((s8[6291456]{0:T(1024)(128)(4,1)}), s8[2097152]{0:T(1024)(128)(4,1)S(1)}, s32[]{:S(2)}) async-start(s8[6291456]{0:T(1024)(128)(4,1)} %bitcast.11), calls=%async_computation.1 | async-start | bytes 4194304
  65.3 13.9 %copy-start.2 = (bf16[256,1024]{1,0:T(8,128)(2,1)S(1)}, bf16[256,1024]{1,0:T(8,128)(2,1)}, u32[]{:S(2)}) copy-start(bf16[256,1024]{1,0:T(8,128)(2,1)} %up_hbm.1) | copy-start | bytes 1572868
  65.3 13.9 %copy-start.3 = (bf16[1024,256]{1,0:T(8,128)(2,1)S(1)}, bf16[1024,256]{1,0:T(8,128)(2,1)}, u32[]{:S(2)}) copy-start(bf16[1024,256]{1,0:T(8,128)(2,1)} %param.21) | copy-start | bytes 1572868
  65.3 13.9 %copy-start.4 = (f32[256]{0:T(256)S(1)}, f32[256]{0:T(256)}, u32[]{:S(2)}) copy-start(f32[256]{0:T(256)} %param.19) | copy-start | bytes 3076
  65.3 13.9 %copy-start.5 = (f32[256]{0:T(256)S(1)}, f32[256]{0:T(256)}, u32[]{:S(2)}) copy-start(f32[256]{0:T(256)} %param.22) | copy-start | bytes 3076
